TPU v7x, 32 devices: a whole 2x2x4 slice. The times are simulated.
32 devices in a mesh: grp: 2 (over y), tm: 4 (over z), tmpl: 2 (over x), chan: 2 (over core).
Axes of the slice: x: 2, y: 2, z: 4, core: 2. Of those that a mesh axis runs over, the one named last changes fastest.
Arguments:
- record: bfloat16 [32, 4096], P('chan', ('grp', 'tm')), parts along dimension 1, may hold values from -640 to 640
- templates: bfloat16 [2, 768, 32, 512], P('tmpl', 'tm', 'chan'), may hold values from -0.046875 to 0.046875
- span_list: int32 [8, 4], P(('grp', 'tm')), parts along dimension 0, may hold values from -1 to 3, as said below
Outputs:
- scan_out: float32 [1536, 4096], P(('tmpl', 'chan'), ('grp', 'tm')), parts along dimension 1
There are 2 independent parts, one for each index of `grp`. A program takes and returns all parts, laid end to end along the dimension named above; an argument that names none is the same for every part. Nothing has to cross between parts.
Inputs may be any that keep to these rules, and one draw needn't show every extreme that they name: `span_list`: each shard lists distinct blocks in its first slots and -1 in the rest; between 1 and 4 blocks a shard, exactly 8 in all shards together, and some shard lists 4.
All inputs are finite; a program needn't handle non-finite values.
Results may differ from a plain program's by a relative error of at most 0.0003.
Values may be sent and summed in bfloat16 or wider, within the bound.
A program may use at most 64 MiB of HBM per device.

v0:
```python
import jax
import jax.numpy as jnp
from jax import lax
from jax.sharding import PartitionSpec as P

C = 32
L = 512
SPAN = 128
MOST_DENSE = 4


def from_behind(block, axis, distance):
    devices = range(lax.axis_size(axis))
    route = [(i - distance, i) for i in devices if i - distance in devices]
    return lax.ppermute(block, axis, route)


def windows(segment):
    seg_len = segment.shape[1]
    tiled = jnp.tile(segment, (1, SPAN + 1))
    flattened = tiled[:, : SPAN * (seg_len + 1)]
    return flattened.reshape(segment.shape[0], SPAN, seg_len + 1)[:, :, :L]


def slot_windows(extended, own_list):
    stacked = []
    for slot in range(MOST_DENSE):
        span_at = own_list[slot]
        segment = lax.dynamic_slice_in_dim(extended, jnp.maximum(span_at, 0) * SPAN, SPAN + L, 1)
        stacked.append(jnp.where(span_at >= 0, windows(segment), jnp.zeros((), extended.dtype)))
    return jnp.stack(stacked)


def local(record, templates, span_list):
    own_list = span_list[0]
    following = from_behind(record, "tm", -1)
    extended = jnp.concatenate([record, following], axis=1)
    own_windows = slot_windows(extended, own_list)
    product = jnp.einsum(
        "kcl,qcrl->kqr",
        lax.all_gather(templates, "tm", axis=1, tiled=True)[0],
        own_windows,
        preferred_element_type=jnp.float32,
    )
    product = product.reshape(product.shape[0], MOST_DENSE * SPAN)
    summed = lax.psum_scatter(product, "chan", scatter_dimension=0, tiled=True)
    local_energy = jnp.sum(jnp.square(own_windows.astype(jnp.float32)), axis=(1, 3)).reshape(-1)
    energy = lax.psum(local_energy, "chan")
    return summed * lax.rsqrt(energy / (C * L) + 1e-05)[None, :]


def solution(mesh):
    in_specs = (P("chan", ("grp", "tm")), P("tmpl", "tm", "chan", None), P(("grp", "tm"), None))
    out_specs = P(("tmpl", "chan"), ("grp", "tm"))
    return jax.shard_map(local, mesh=mesh, in_specs=in_specs, out_specs=out_specs, check_vma=False)
```

profile of v0, /device:TPU:0, one launch (start us, length us, event | category | flops | bytes accessed | tf_op | source)
XLA Modules:
  0.0 266.6 jit_solution(5071008891932363301)
XLA Ops:
  6.5 0.0 all-gather.2.cloned.1.call-start
  6.5 5.3 %copy.6 = bf16[1,192,16,512]{3,1,2,0:T(8,128)(2,1)} copy(bf16[1,192,16,512]{3,2,1,0:T(8,128)(2,1)} %param.4) | data formatting | bytes 6291456 | tf_op args[1]
  11.8 0.0 copy-start.2
  11.8 0.0 copy-start.3
  11.8 0.0 all-gather.2.cloned.1.call-update
  11.8 0.0 reduce-scatter.2.cloned.1.call-start
  11.9 0.6 copy-done.2
  12.5 1.3 collective-permute-start
  13.8 0.0 copy-done.3
  13.8 0.7 fusion.7
  19.8 0.0 collective-permute-done
  19.8 0.2 tile.16
  20.0 0.3 copy.9
  20.4 0.2 slice.52
  20.6 8.1 %reshape.67 = bf16[16,128,641]{2,1,0:T(8,128)(2,1)} reshape(bf16[16,82048]{1,0:T(8,128)(2,1)S(1)} %slice.52) | data formatting | bytes 5251072 | tf_op jit(solution)/shard_map/reshape | solution.py:22
  28.6 0.2 tile.42
  28.9 0.3 copy.12
  29.2 0.2 slice.58
  29.4 7.9 %reshape.70 = bf16[16,128,641]{2,1,0:T(8,128)(2,1)} reshape(bf16[16,82048]{1,0:T(8,128)(2,1)S(1)} %slice.58) | data formatting | bytes 5251072 | tf_op jit(solution)/shard_map/reshape | solution.py:22
  37.3 0.2 tile.40
  37.5 0.3 copy.11
  37.8 0.2 slice.56
  38.0 7.9 %reshape.69 = bf16[16,128,641]{2,1,0:T(8,128)(2,1)} reshape(bf16[16,82048]{1,0:T(8,128)(2,1)S(1)} %slice.56) | data formatting | bytes 5251072 | tf_op jit(solution)/shard_map/reshape | solution.py:22
  45.9 0.2 tile.18
  46.1 0.3 copy.10
  46.4 0.2 slice.54
  46.6 8.1 %reshape.68 = bf16[16,128,641]{2,1,0:T(8,128)(2,1)} reshape(bf16[16,82048]{1,0:T(8,128)(2,1)S(1)} %slice.54) | data formatting | bytes 5251072 | tf_op jit(solution)/shard_map/reshape | solution.py:22
  54.7 0.0 copy-start
  54.7 0.0 copy-start.1
  54.7 4.1 %fusion.2 = (bf16[1,16,128,512]{3,2,1,0:T(8,128)(2,1)S(1)}, bf16[1,16,128,512]{3,2,1,0:T(8,128)(2,1)}) fusion(bf16[16,128,641]{2,1,0:T(8,128)(2,1)} %reshape.70, pred[]{:T(512)} %bitcast.9, bf16[16,128,641]{2,1,0:T(8,128)(2,1)} %reshape.69, pred[]{:T(512)} %bitcast.6), kind=kLoop, calls=%fused_computation.5 | loop fusion | flops 2097152 | bytes 8388610 | tf_op jit(solution)/shard_map/stack | solution.py:31
  58.8 0.0 copy-done
  58.8 0.8 copy-done.1
  59.7 2.2 fusion.4
  61.9 171.0 %all-gather.2.cloned.1.call-done = bf16[1,768,16,512]{3,1,2,0:T(8,128)(2,1)} async-done(((bf16[1,192,16,512]{3,1,2,0:T(8,128)(2,1)}), bf16[1,768,16,512]{3,1,2,0:T(8,128)(2,1)}) %all-gather.2.cloned.1.call-update) | async-done | bytes 12582928 | tf_op jit(solution)/shard_map/all_gather | solution.py:41
  232.9 14.3 %fusion = f32[4,128,768,1]{2,1,3,0:T(8,128)} fusion(bf16[1,768,16,512]{3,1,2,0:T(8,128)(2,1)} %all-gather.2.cloned.1.call-done, bf16[1,16,128,512]{3,2,1,0:T(8,128)(2,1)S(1)} %get-tuple-element.13, bf16[1,16,128,512]{3,2,1,0:T(8,128)(2,1)} %get-tuple-element.14, bf16[1,16,128,512]{3,2,1,0:T(8,128)(2,1)} %get-tuple-element.15, ...), kind=kOutput, calls=%fused_computation.1 | convolution fusion | flops 6455033856 | bytes 22544384 | tf_op jit(solution)/shard_map/kcl,qcrl->kqr/dot_general | solution.py:39
  247.2 3.0 %copy.7 = f32[768,512]{1,0:T(8,128)} copy(f32[768,512]{0,1:T(8,128)} %bitcast.43) | data formatting | bytes 3145728 | tf_op jit(solution)/shard_map/reshape | solution.py:45
  250.3 0.0 reduce-scatter.2.cloned.1.call-update
  250.3 4.3 %multiply_reduce_fusion = f32[4,128]{1,0:T(4,128)S(1)} fusion(bf16[1,16,128,512]{3,2,1,0:T(8,128)(2,1)S(1)} %get-tuple-element.13, bf16[1,16,128,512]{3,2,1,0:T(8,128)(2,1)} %get-tuple-element.14, bf16[1,16,128,512]{3,2,1,0:T(8,128)(2,1)} %get-tuple-element.15, bf16[1,16,128,512]{3,2,1,0:T(8,128)(2,1)} %get-tuple-element.16), kind=kLoop, calls=%fused_computation | loop fusion | flops 25165312 | bytes 8390656 | tf_op jit(solution)/shard_map/reduce_sum | solution.py:47
  254.6 2.5 psum.7
  257.1 0.6 reduce-scatter.2.cloned.1.call-done
  257.7 2.1 broadcast_multiply_fusion
  (4 shorter events, 0.0 us)
Async XLA Ops:
  6.5 226.4 %all-gather.2.cloned.1.call-start = ((), (), s32[]{:S(2)}) async-start(), calls=%async_computation.1 | async-start | bytes 15728640 | tf_op jit(solution)/shard_map/all_gather | solution.py:41
  11.8 0.7 copy-start.2
  11.8 2.0 copy-start.3
  11.8 245.8 %reduce-scatter.2.cloned.1.call-start = ((), (), s32[]{:S(2)}) async-start(), calls=%async_computation.2 | async-start | bytes 2359296 | tf_op jit(solution)/shard_map/reduce_scatter | solution.py:46
  12.5 7.2 %collective-permute-start = (bf16[16,512]{1,0:T(8,128)(2,1)S(1)}, bf16[16,512]{1,0:T(8,128)(2,1)S(1)}, u32[]{:S(2)}, u32[]{:S(2)}) collective-permute-start(bf16[16,512]{1,0:T(8,128)(2,1)S(1)} %copy-done.2), channel_id=1, source_target_pairs={{4,0},{8,4},{12,8},{5,1},{9,5},{13,9},{6,2},{10,6},{14,10},{7,3},{... | collective-permute-start | bytes 49160 | tf_op jit(solution)/shard_map/ppermute | solution.py:15
  54.7 4.1 %copy-start = (bf16[16,128,641]{2,1,0:T(8,128)(2,1)S(1)}, bf16[16,128,641]{2,1,0:T(8,128)(2,1)}, u32[]{:S(2)}) copy-start(bf16[16,128,641]{2,1,0:T(8,128)(2,1)} %reshape.67) | copy-start | bytes 7876612
  54.7 4.9 %copy-start.1 = (bf16[16,128,641]{2,1,0:T(8,128)(2,1)S(1)}, bf16[16,128,641]{2,1,0:T(8,128)(2,1)}, u32[]{:S(2)}) copy-start(bf16[16,128,641]{2,1,0:T(8,128)(2,1)} %reshape.68) | copy-start | bytes 7876612
Sparse Core Ops, SparseCore 0:
  12.0 220.8 all-gather.1
  250.4 7.2 reduce-scatter.1
where the time goes:
time: 267 us
  waiting for transfers between devices  172 us (64%)
  local copies, waits for them, and re-layouts  45.3 us (17%)
  between operations  18.8 us (7%)
  matrix products  14.3 us (5%)
  other arithmetic  12.8 us (5%)
    all_gather x1, waiting for transfers between devices, local(): lax.all_gather(templates, 'tm', axis=1, tiled=True)[0]  171 us
    reshape x4, local copies, waits for them, and re-layouts, windows(): return flattened.reshape(segment.shape[0], SPAN, seg_len + 1)[:, :, :L]  31.9 us
    dot_general x1, matrix products, local(): jnp.einsum('kcl,qcrl->kqr', lax.all_gather(templates, 'tm', axis=1, tiled...  14.3 us
    unnamed x14, local copies, waits for them, and re-layouts  8.11 us
    another operation x2, other arithmetic, slot_windows(): return jnp.stack(stacked)  6.34 us
  transfers between devices with their start and end apart: 3, of which 2 were waited for; matrix products, arithmetic and copies ran while one was open for 17% of the time, Pallas kernels for 0%

commit v1 on v0

--- a/solution.py
+++ b/solution.py
@@ -7,6 +7,22 @@
 L = 512
 SPAN = 128
 MOST_DENSE = 4
+
+
+def collect(x, axis, dim):
+    ways, here, step = (lax.axis_size(axis), lax.axis_index(axis), x.shape[dim])
+    dims = [n * ways if d == dim else n for d, n in enumerate(x.shape)]
+    full = lax.dynamic_update_slice_in_dim(jnp.zeros(dims, x.dtype), x, here * step, axis=dim)
+    going_up = going_down = x
+    for far in range(1, ways // 2 + 1):
+        going_up = lax.ppermute(going_up, axis, [(d, (d + 1) % ways) for d in range(ways)])
+        full = lax.dynamic_update_slice_in_dim(full, going_up, (here - far) % ways * step, axis=dim)
+        if 2 * far < ways:
+            going_down = lax.ppermute(going_down, axis, [(d, (d - 1) % ways) for d in range(ways)])
+            full = lax.dynamic_update_slice_in_dim(
+                full, going_down, (here + far) % ways * step, axis=dim
+            )
+    return full
 
 
 def from_behind(block, axis, distance):
@@ -38,7 +54,7 @@
     own_windows = slot_windows(extended, own_list)
     product = jnp.einsum(
         "kcl,qcrl->kqr",
-        lax.all_gather(templates, "tm", axis=1, tiled=True)[0],
+        collect(templates, "tm", 1)[0],
         own_windows,
         preferred_element_type=jnp.float32,
     )

time: 267 us -> 305 us (1.14)
  local copies, waits for them, and re-layouts: 45.3 us -> 68.1 us
  waiting for transfers between devices: 172 us -> 187 us
  starting transfers between devices: 1.32 us -> 6.34 us
  other arithmetic: 12.8 us -> 9.33 us
    all_gather x1 -> x0, waiting for transfers between devices: 171 us -> none  [local(): lax.all_gather(templates, 'tm', axis=1, tiled=True)[0]]
    ppermute x1, waiting for transfers between devices: 0.01 us -> 115 us  [from_behind(): return lax.ppermute(block, axis, route)]
    ppermute x0 -> x3, waiting for transfers between devices: none -> 69.3 us  [the longest x2 69.3 us: collect(): lax.ppermute(going_up, axis, [(d, (d + 1) % ways) for d in range(ways)])]
    dynamic_update_slice x0 -> x4, local copies, waits for them, and re-layouts: none -> 20.9 us  [the longest x2 12.1 us: collect(): lax.dynamic_update_slice_in_dim(full, going_up, (here - far) % ways * ste...]
    squeeze x0 -> x1, local copies, waits for them, and re-layouts: none -> 5.74 us  [local(): collect(templates, 'tm', 1)[0]]
    ppermute x0 -> x3, starting transfers between devices: none -> 5.05 us  [the longest x2 3.03 us: collect(): lax.ppermute(going_up, axis, [(d, (d + 1) % ways) for d in range(ways)])]
    unnamed x14 -> x19, local copies, waits for them, and re-layouts: 8.11 us -> 4.28 us
    another operation x2, other arithmetic: 6.34 us -> 2.92 us  [slot_windows(): return jnp.stack(stacked)]
  transfers between devices with their start and end apart: 3 -> 5, of which waited for: 2 -> 3; matrix products, arithmetic and copies ran while one was open for 17% -> 21% of each run, Pallas kernels for 0% -> 0%
where the time goes in v1:
time: 305 us
  waiting for transfers between devices  187 us (61%)
  local copies, waits for them, and re-layouts  68.1 us (22%)
  between operations  18.8 us (6%)
  matrix products  12.4 us (4%)
  other arithmetic  9.33 us (3%)
  starting transfers between devices  6.34 us (2%)
    ppermute x1, waiting for transfers between devices, from_behind(): return lax.ppermute(block, axis, route)  115 us
    ppermute x2, waiting for transfers between devices, collect(): lax.ppermute(going_up, axis, [(d, (d + 1) % ways) for d in range(ways)])  69.3 us
    reshape x4, local copies, waits for them, and re-layouts, windows(): return flattened.reshape(segment.shape[0], SPAN, seg_len + 1)[:, :, :L]  31.9 us
    dot_general x1, matrix products, local(): jnp.einsum('kcl,qcrl->kqr', collect(templates, 'tm', 1)[0], own_windows,...  12.4 us
    dynamic_update_slice x2, local copies, waits for them, and re-layouts, collect(): lax.dynamic_update_slice_in_dim(full, going_up, (here - far) % ways * ste...  12.1 us
  transfers between devices with their start and end apart: 5, of which 3 were waited for; matrix products, arithmetic and copies ran while one was open for 21% of the time, Pallas kernels for 0%

profile of v1, /device:TPU:0, one launch (start us, length us, event | category | flops | bytes accessed | tf_op | source)
XLA Modules:
  0.0 304.5 jit_solution(14031956946285210062)
XLA Ops:
  6.5 0.0 reduce-scatter.2.cloned.1.call-start
  6.5 3.0 collective-permute-start
  9.6 2.0 collective-permute-start.1
  11.6 69.3 %collective-permute-done = bf16[1,192,16,512]{3,2,1,0:T(8,128)(2,1)} collective-permute-done((bf16[1,192,16,512]{3,2,1,0:T(8,128)(2,1)}, bf16[1,192,16,512]{3,2,1,0:T(8,128)(2,1)}, u32[]{:S(2)}, u32[]{:S(2)}) %collective-permute-start) | collective-permute-done | bytes 3145760 | tf_op jit(solution)/shard_map/ppermute | solution.py:18
  80.9 0.0 collective-permute-start.2
  80.9 1.3 collective-permute-start.3
  82.2 0.7 constant_dynamic-update-slice_fusion.1
  82.9 5.7 %squeeze.16 = bf16[768,16,512]{2,0,1:T(8,128)(2,1)} broadcast(bf16[]{:T(256)} %constant.52.clone.1), dimensions={} | broadcast | bytes 12582914 | tf_op jit(solution)/shard_map/squeeze | solution.py:57
  88.6 3.4 %copy_dynamic-update-slice_fusion.3 = bf16[768,16,512]{2,0,1:T(8,128)(2,1)} fusion(bf16[768,16,512]{2,0,1:T(8,128)(2,1)} %squeeze.16, s32[]{:T(128)S(6)} %select_n.65, bf16[192,16,512]{2,1,0:T(8,128)(2,1)S(1)} %bitcast.44), kind=kLoop, calls=%fused_computation.7 | loop fusion | bytes 6291460 | tf_op jit(solution)/shard_map/dynamic_update_slice | solution.py:15
  92.0 0.0 copy-done.6
  92.0 0.7 fusion.7
  98.0 114.7 %collective-permute-done.3 = bf16[16,512]{1,0:T(8,128)(2,1)S(1)} collective-permute-done((bf16[16,512]{1,0:T(8,128)(2,1)}, bf16[16,512]{1,0:T(8,128)(2,1)S(1)}, u32[]{:S(2)}, u32[]{:S(2)}) %collective-permute-start.3) | collective-permute-done | bytes 16416 | tf_op jit(solution)/shard_map/ppermute | solution.py:31
  212.7 0.2 tile.40
  212.9 0.3 copy.17
  213.3 0.2 slice.56
  213.5 8.0 %reshape.77 = bf16[16,128,641]{2,1,0:T(8,128)(2,1)} reshape(bf16[16,82048]{1,0:T(8,128)(2,1)S(1)} %slice.56) | data formatting | bytes 5251072 | tf_op jit(solution)/shard_map/reshape | solution.py:38
  221.5 0.2 tile.42
  221.7 0.3 copy.18
  222.1 0.2 slice.58
  222.2 7.9 %reshape.78 = bf16[16,128,641]{2,1,0:T(8,128)(2,1)} reshape(bf16[16,82048]{1,0:T(8,128)(2,1)S(1)} %slice.58) | data formatting | bytes 5251072 | tf_op jit(solution)/shard_map/reshape | solution.py:38
  230.1 0.2 tile.16
  230.3 0.3 copy.15
  230.7 0.2 slice.52
  230.8 7.8 %reshape.75 = bf16[16,128,641]{2,1,0:T(8,128)(2,1)} reshape(bf16[16,82048]{1,0:T(8,128)(2,1)S(1)} %slice.52) | data formatting | bytes 5251072 | tf_op jit(solution)/shard_map/reshape | solution.py:38
  238.7 0.2 tile.18
  238.9 0.3 copy.16
  239.3 0.2 slice.54
  239.4 8.1 %reshape.76 = bf16[16,128,641]{2,1,0:T(8,128)(2,1)} reshape(bf16[16,82048]{1,0:T(8,128)(2,1)S(1)} %slice.54) | data formatting | bytes 5251072 | tf_op jit(solution)/shard_map/reshape | solution.py:38
  247.6 2.6 fusion.2
  250.2 0.5 copy-done
  250.7 1.7 copy-done.1
  252.4 0.3 fusion.4
  252.7 0.0 copy-start.3
  252.7 0.0 copy-start.4
  252.7 6.8 %copy_dynamic-update-slice_fusion.2 = bf16[768,16,512]{2,0,1:T(8,128)(2,1)} fusion(bf16[768,16,512]{2,0,1:T(8,128)(2,1)} %copy_dynamic-update-slice_fusion.3, s32[]{:T(128)S(6)} %select_n.67, bf16[192,16,512]{2,1,0:T(8,128)(2,1)} %bitcast.1), kind=kLoop, calls=%fused_computation.6 | loop fusion | bytes 6291460 | tf_op jit(solution)/shard_map/dynamic_update_slice | solution.py:19
  259.5 0.0 collective-permute-done.1
  259.5 5.4 %copy_dynamic-update-slice_fusion.1 = bf16[768,16,512]{2,0,1:T(8,128)(2,1)} fusion(bf16[768,16,512]{2,0,1:T(8,128)(2,1)} %copy_dynamic-update-slice_fusion.2, s32[]{:T(128)S(6)} %select_n.69, bf16[192,16,512]{2,1,0:T(8,128)(2,1)} %bitcast.2), kind=kLoop, calls=%fused_computation.5 | loop fusion | bytes 6291460 | tf_op jit(solution)/shard_map/dynamic_update_slice | solution.py:22
  264.9 0.0 collective-permute-done.2
  264.9 5.3 %copy_dynamic-update-slice_fusion = bf16[768,16,512]{2,0,1:T(8,128)(2,1)} fusion(bf16[768,16,512]{2,0,1:T(8,128)(2,1)} %copy_dynamic-update-slice_fusion.1, s32[]{:T(128)S(6)} %select_n.71, bf16[192,16,512]{2,1,0:T(8,128)(2,1)} %bitcast.3), kind=kLoop, calls=%fused_computation.4 | loop fusion | bytes 6291460 | tf_op jit(solution)/shard_map/dynamic_update_slice | solution.py:19
  270.2 0.0 copy-done.2
  270.2 0.0 copy-done.4
  270.2 12.4 %fusion = f32[768,4,128,1]{0,2,3,1:T(8,128)} fusion(bf16[768,16,512]{2,0,1:T(8,128)(2,1)} %copy_dynamic-update-slice_fusion, bf16[1,16,128,512]{3,2,1,0:T(8,128)(2,1)S(1)} %get-tuple-element.13, bf16[1,16,128,512]{3,2,1,0:T(8,128)(2,1)S(1)} %get-tuple-element.14, bf16[1,16,128,512]{3,2,1,0:T(8,128)(2,1)S(1)} %get-tuple-element.15, ...), kind=kOutput, calls=%fused_computation.1 | convolution fusion | flops 6476005376 | bytes 22544384 | tf_op jit(solution)/shard_map/kcl,qcrl->kqr/dot_general | solution.py:55
  282.7 3.0 copy.13
  285.7 0.0 reduce-scatter.2.cloned.1.call-update
  285.7 4.3 %multiply_reduce_fusion = f32[4,128]{1,0:T(4,128)S(1)} fusion(bf16[1,16,128,512]{3,2,1,0:T(8,128)(2,1)S(1)} %get-tuple-element.13, bf16[1,16,128,512]{3,2,1,0:T(8,128)(2,1)} %copy-done.2, bf16[1,16,128,512]{3,2,1,0:T(8,128)(2,1)} %copy-done.3, bf16[1,16,128,512]{3,2,1,0:T(8,128)(2,1)} %copy-done.4), kind=kLoop, calls=%fused_computation | loop fusion | flops 25165312 | bytes 8390656 | tf_op jit(solution)/shard_map/reduce_sum | solution.py:63
  290.0 2.5 psum.7
  292.5 3.1 %reduce-scatter.2.cloned.1.call-done = f32[384,512]{1,0:T(8,128)} async-done(((f32[768,512]{1,0:T(8,128)}), f32[384,512]{1,0:T(8,128)}) %reduce-scatter.2.cloned.1.call-update) | async-done | bytes 786448 | tf_op jit(solution)/shard_map/reduce_scatter | solution.py:62
  295.6 2.1 broadcast_multiply_fusion
  (10 shorter events, 0.0 us)
Async XLA Ops:
  6.5 289.0 %reduce-scatter.2.cloned.1.call-start = ((), (), s32[]{:S(2)}) async-start(), calls=%async_computation.1 | async-start | bytes 2359296 | tf_op jit(solution)/shard_map/reduce_scatter | solution.py:62
  6.5 74.3 %collective-permute-start = (bf16[1,192,16,512]{3,2,1,0:T(8,128)(2,1)}, bf16[1,192,16,512]{3,2,1,0:T(8,128)(2,1)}, u32[]{:S(2)}, u32[]{:S(2)}) collective-permute-start(bf16[1,192,16,512]{3,2,1,0:T(8,128)(2,1)} %param.4), channel_id=1, source_target_pairs={{0,4},{4,8},{8,12},{12,0},{1,5},{5,9},{9,13},{13,1},{2,6},{6,10},{... | collective-permute-start | bytes 9437192 | tf_op jit(solution)/shard_map/ppermute | solution.py:18
  9.6 250.0 %collective-permute-start.1 = (bf16[1,192,16,512]{3,2,1,0:T(8,128)(2,1)}, bf16[1,192,16,512]{3,2,1,0:T(8,128)(2,1)}, u32[]{:S(2)}, u32[]{:S(2)}) collective-permute-start(bf16[1,192,16,512]{3,2,1,0:T(8,128)(2,1)} %param.4), channel_id=1, source_target_pairs={{0,12},{4,0},{8,4},{12,8},{1,13},{5,1},{9,5},{13,9},{2,14},{6,2},{... | collective-permute-start | bytes 9437192 | tf_op jit(solution)/shard_map/ppermute | solution.py:21
  80.9 184.0 %collective-permute-start.2 = (bf16[1,192,16,512]{3,2,1,0:T(8,128)(2,1)}, bf16[1,192,16,512]{3,2,1,0:T(8,128)(2,1)}, u32[]{:S(2)}, u32[]{:S(2)}) collective-permute-start(bf16[1,192,16,512]{3,2,1,0:T(8,128)(2,1)} %collective-permute-done), channel_id=1, source_target_pairs={{0,4},{4,8},{8,12},{12,0},{1,5},{5,9},{9,13},{13,1},{2,6},{6,10},{... | collective-permute-start | bytes 9437192 | tf_op jit(solution)/shard_map/ppermute | solution.py:18
  80.9 131.8 %collective-permute-start.3 = (bf16[16,512]{1,0:T(8,128)(2,1)}, bf16[16,512]{1,0:T(8,128)(2,1)S(1)}, u32[]{:S(2)}, u32[]{:S(2)}) collective-permute-start(bf16[16,512]{1,0:T(8,128)(2,1)} %param.3), channel_id=1, source_target_pairs={{4,0},{8,4},{12,8},{5,1},{9,5},{13,9},{6,2},{10,6},{14,10},{7,3},{... | collective-permute-start | bytes 49160 | tf_op jit(solution)/shard_map/ppermute | solution.py:31
  82.9 5.7 %copy-start.5 = (bf16[1,192,16,512]{3,2,1,0:T(8,128)(2,1)S(1)}, bf16[1,192,16,512]{3,2,1,0:T(8,128)(2,1)}, u32[]{:S(2)}) copy-start(bf16[1,192,16,512]{3,2,1,0:T(8,128)(2,1)} %param.4) | copy-start | bytes 9437188
  88.6 3.4 %copy-start.6 = (s32[1,4]{1,0:T(1,128)S(1)}, s32[1,4]{1,0:T(1,128)}, u32[]{:S(2)}) copy-start(s32[1,4]{1,0:T(1,128)} %param.5) | copy-start | bytes 52
  247.6 3.2 %copy-start = (bf16[16,128,641]{2,1,0:T(8,128)(2,1)S(1)}, bf16[16,128,641]{2,1,0:T(8,128)(2,1)}, u32[]{:S(2)}) copy-start(bf16[16,128,641]{2,1,0:T(8,128)(2,1)} %reshape.75) | copy-start | bytes 7876612
  247.6 4.9 %copy-start.1 = (bf16[16,128,641]{2,1,0:T(8,128)(2,1)S(1)}, bf16[16,128,641]{2,1,0:T(8,128)(2,1)}, u32[]{:S(2)}) copy-start(bf16[16,128,641]{2,1,0:T(8,128)(2,1)} %reshape.76) | copy-start | bytes 7876612
  250.2 20.0 %copy-start.2 = (bf16[1,16,128,512]{3,2,1,0:T(8,128)(2,1)}, bf16[1,16,128,512]{3,2,1,0:T(8,128)(2,1)S(1)}, u32[]{:S(2)}) copy-start(bf16[1,16,128,512]{3,2,1,0:T(8,128)(2,1)S(1)} %get-tuple-element.14) | copy-start | bytes 6291460
  252.7 17.5 %copy-start.3 = (bf16[1,16,128,512]{3,2,1,0:T(8,128)(2,1)}, bf16[1,16,128,512]{3,2,1,0:T(8,128)(2,1)S(1)}, u32[]{:S(2)}) copy-start(bf16[1,16,128,512]{3,2,1,0:T(8,128)(2,1)S(1)} %get-tuple-element.15) | copy-start | bytes 6291460
  252.7 17.5 %copy-start.4 = (bf16[1,16,128,512]{3,2,1,0:T(8,128)(2,1)}, bf16[1,16,128,512]{3,2,1,0:T(8,128)(2,1)S(1)}, u32[]{:S(2)}) copy-start(bf16[1,16,128,512]{3,2,1,0:T(8,128)(2,1)S(1)} %get-tuple-element.16) | copy-start | bytes 6291460
Sparse Core Ops, SparseCore 0:
  285.8 9.6 reduce-scatter.1
